TPU v7x, 256 devices: a whole 4x4x8 slice. The times are simulated.
256 devices in a mesh: dp: 32 (over z, x_hi, core), row: 4 (over y), col: 2 (over x_lo).
Axes of the slice: x: 4 (x_hi: 2, x_lo: 2; x = x_hi * 2 + x_lo), y: 4, z: 8, core: 2. Of those that a mesh axis runs over, the one named last changes fastest.
Arguments:
- tokens: bfloat16 [6144, 4096], P('dp', ('row', 'col')), may hold values from -6 to 6
- in_weight: bfloat16 [4096, 3, 4096], P('dp', None, ('row', 'col')), may hold values from -0.09375 to 0.09375
- short_filter: float32 [3, 3, 4096], P(None, None, ('row', 'col')), may hold values from -3 to 3
- long_filter: bfloat16 [256, 128], P(('row', 'col')), may hold values from -0.59765625 to 0.59765625
- grad_out: bfloat16 [6144, 4096], P('dp', ('row', 'col')), may hold values from -6 to 6
Outputs:
- mixed: bfloat16 [6144, 4096], P('dp', ('row', 'col'))
- grad_in: bfloat16 [6144, 4096], P('dp', ('row', 'col'))
- grad_weight: float32 [4096, 3, 4096], P('dp', None, ('row', 'col'))
- grad_long: float32 [256, 128], P(('row', 'col'))
- grad_short: float32 [3, 3, 4096], P(None, None, ('row', 'col'))
All inputs are finite; a program needn't handle non-finite values.
Results may differ from a plain program's by a relative error of at most 0.019.
Values may be sent and summed in bfloat16 or wider, within the bound.
A program may use at most 128 MiB of HBM per device.

v0:
```python
import jax
import jax.numpy as jnp
from jax import lax
from jax.sharding import PartitionSpec as P


def from_behind(block, axis, distance):
    devices = range(lax.axis_size(axis))
    route = [(i - distance, i) for i in devices if i - distance in devices]
    return lax.ppermute(block, axis, route)


def toeplitz(leading, rows, span):
    groups = leading.shape[0]
    width = rows + span
    seed_row = jnp.concatenate(
        [leading, jnp.zeros((groups, width - leading.shape[1]), leading.dtype)], axis=1
    )
    tiled = jnp.tile(seed_row, (1, rows))
    skewed = tiled[:, : rows * (width - 1)].reshape(groups, rows, width - 1)
    return skewed[:, :, :span]


def to_groups(values, ngroups, members):
    count = values.shape[0]
    return values.reshape(count, ngroups, members).transpose(1, 2, 0)


def from_groups(values):
    groups, members, count = values.shape
    return values.transpose(2, 0, 1).reshape(count, groups * members)


def per_device(tokens, in_weight, short_filter, long_filter, grad_out):
    rows = tokens.shape[0]
    local = grad_out.shape[1]
    nshort = short_filter.shape[0]
    ntaps = long_filter.shape[1]
    ngroups = long_filter.shape[0]
    members = local // ngroups
    margin = ntaps - 1
    span = rows + margin
    scale = float(rows * lax.axis_size("dp")) ** (-0.5)
    whole = lax.all_gather(tokens, ("row", "col"), axis=1, tiled=True)
    full_w = lax.all_gather(in_weight, "dp", axis=0, tiled=True)
    mixed_in = jnp.einsum("sd,dic->sic", whole, full_w, preferred_element_type=jnp.float32).astype(
        jnp.bfloat16
    )
    before = from_behind(mixed_in[rows - margin - nshort + 1 :], "dp", 1)
    extended = jnp.concatenate([before, mixed_in], axis=0).astype(jnp.float32)
    long_feats = jnp.zeros((span, 3, local), jnp.float32)
    for j in range(nshort):
        long_feats = (
            long_feats + short_filter[j][None] * extended[nshort - 1 - j : nshort - 1 - j + span]
        )
    product_ext = (long_feats[:, 1] * long_feats[:, 2]).astype(jnp.bfloat16)
    feats = long_feats[margin:]
    short_rows = extended[margin:]
    product_cols = to_groups(product_ext, ngroups, members)
    causal = toeplitz(long_filter[:, ::-1], rows, span)
    conv = from_groups(
        jnp.einsum("gst,gct->gcs", causal, product_cols, preferred_element_type=jnp.float32)
    )
    mixed = (feats[:, 0] * conv).astype(jnp.bfloat16)
    upstream = grad_out.astype(jnp.float32)
    grad_query = upstream * conv
    grad_conv = (upstream * feats[:, 0]).astype(jnp.bfloat16)
    after = from_behind(grad_conv[:margin], "dp", -1)
    grad_ext = jnp.concatenate([grad_conv, after], axis=0)
    anti = toeplitz(long_filter, rows, span)
    grad_product = from_groups(
        jnp.einsum(
            "gst,gct->gcs",
            anti,
            to_groups(grad_ext, ngroups, members),
            preferred_element_type=jnp.float32,
        )
    )
    reversed_cols = jnp.concatenate(
        [product_cols[:, :, ::-1], jnp.zeros((ngroups, members, rows), product_cols.dtype)], axis=2
    )
    width = span + rows
    pairs = jnp.einsum(
        "gcs,gcu->gsu",
        to_groups(grad_conv, ngroups, members),
        reversed_cols,
        preferred_element_type=jnp.float32,
    )
    diagonal = pairs.reshape(ngroups, rows * width)[:, : rows * (width - 1)].reshape(
        ngroups, rows, width - 1
    )
    filter_part = jnp.sum(diagonal[:, :, rows - 1 : rows - 1 + ntaps], axis=1)
    grad_feats = jnp.stack(
        [grad_query, grad_product * feats[:, 2], grad_product * feats[:, 1]], axis=1
    )
    later = from_behind(grad_feats[: nshort - 1], "dp", -1)
    feats_ext = jnp.concatenate([grad_feats, later], axis=0)
    grad_acc = jnp.zeros((rows, 3, local), jnp.float32)
    for j in range(nshort):
        grad_acc = grad_acc + short_filter[j][None] * feats_ext[j : j + rows]
    grad_mixed = grad_acc.astype(jnp.bfloat16)
    short_part = jnp.stack(
        [
            jnp.sum(grad_feats * short_rows[nshort - 1 - j : nshort - 1 - j + rows], axis=0)
            for j in range(nshort)
        ]
    )
    filter_total, short_total = (
        lax.psum(filter_part.astype(jnp.bfloat16), "dp").astype(jnp.float32),
        lax.psum(short_part.astype(jnp.bfloat16), "dp").astype(jnp.float32),
    )
    grad_long = filter_total * scale
    grad_short = short_total * scale
    partial_in = jnp.einsum("sic,dic->sd", grad_mixed, full_w, preferred_element_type=jnp.float32)
    summed_in = lax.psum_scatter(
        partial_in.astype(jnp.bfloat16), ("row", "col"), scatter_dimension=1, tiled=True
    )
    weight_term = (
        jnp.einsum("sd,sic->dic", whole, grad_mixed, preferred_element_type=jnp.float32) * scale
    )
    grad_weight = lax.psum_scatter(
        weight_term.astype(jnp.bfloat16), "dp", scatter_dimension=0, tiled=True
    ).astype(jnp.float32)
    return (mixed, summed_in, grad_weight, grad_long, grad_short)


def solution(mesh):
    placed = (
        P("dp", ("row", "col")),
        P("dp", None, ("row", "col")),
        P(None, None, ("row", "col")),
        P(("row", "col"), None),
        P("dp", ("row", "col")),
    )
    return jax.shard_map(
        per_device,
        mesh=mesh,
        in_specs=placed,
        out_specs=(
            P("dp", ("row", "col")),
            P("dp", ("row", "col")),
            P("dp", None, ("row", "col")),
            P(("row", "col"), None),
            P(None, None, ("row", "col")),
        ),
        check_vma=False,
    )
```

profile of v0, /device:TPU:4, one launch (start us, length us, event | category | flops | bytes accessed | tf_op | source)
XLA Modules:
  0.0 539.4 jit_solution(406576866576352220)
XLA Ops:
  7.2 0.0 all-gather.3.cloned.1.call-start
  7.2 0.7 all-gather.3.cloned.1.call-update
  7.9 0.0 all-gather.5.cloned.1.call-start
  7.9 0.7 all-gather.5.cloned.1.call-update
  8.7 0.0 reduce-scatter.7.cloned.1.call-start
  8.7 48.7 %all-gather.3.cloned.1.call-done = bf16[192,4096]{1,0:T(8,128)(2,1)} async-done(((bf16[192,512]{1,0:T(8,128)(2,1)}), bf16[192,4096]{1,0:T(8,128)(2,1)}) %all-gather.3.cloned.1.call-update) | async-done | bytes 1572880 | tf_op jit(solution)/shard_map/all_gather | solution.py:44
  57.4 117.2 %all-gather.5.cloned.1.call-done = bf16[4096,3,512]{2,0,1:T(8,128)(2,1)} async-done(((bf16[128,3,512]{2,0,1:T(8,128)(2,1)}), bf16[4096,3,512]{2,0,1:T(8,128)(2,1)}) %all-gather.5.cloned.1.call-update) | async-done | bytes 12582928 | tf_op jit(solution)/shard_map/all_gather | solution.py:45
  174.6 7.7 %fusion.10 = bf16[192,3,512]{2,0,1:T(8,128)(2,1)S(1)} fusion(bf16[4096,3,512]{2,0,1:T(8,128)(2,1)} %all-gather.5.cloned.1.call-done, bf16[192,4096]{1,0:T(8,128)(2,1)} %all-gather.3.cloned.1.call-done), kind=kOutput, calls=%fused_computation.16 | convolution fusion | flops 2416214016 | bytes 14745600 | tf_op jit(solution)/shard_map/sd,dic->sic/dot_general | solution.py:46
  182.3 0.1 slice.112
  182.4 2.2 collective-permute-start
  184.6 0.1 rev.6
  184.7 3.1 tile.8
  187.8 11.6 %tile.9 = bf16[32,98112]{1,0:T(8,128)(2,1)} reshape(bf16[32,192,511]{2,1,0:T(8,128)(2,1)} %tile.8) | data formatting | bytes 12558336 | tf_op jit(solution)/shard_map/tile | solution.py:19
  199.4 5.8 %slice.119 = bf16[32,97920]{1,0:T(8,128)(2,1)} slice(bf16[32,98112]{1,0:T(8,128)(2,1)} %tile.9), slice={[0:32], [0:97920]} | slice | bytes 12533760 | tf_op jit(solution)/shard_map/slice | solution.py:20
  205.3 15.3 %reshape.49 = bf16[32,192,510]{2,1,0:T(8,128)(2,1)} reshape(bf16[32,97920]{1,0:T(8,128)(2,1)} %slice.119) | data formatting | bytes 12533760 | tf_op jit(solution)/shard_map/reshape | solution.py:20
  220.6 0.0 collective-permute-done
  220.6 0.3 maximum_convert_fusion
  220.9 0.6 fusion.5
  221.5 0.0 copy-start
  221.5 1.3 copy-done
  222.8 0.1 fusion.19
  222.8 0.2 copy.24
  223.1 0.0 copy-start.3
  223.1 4.1 fusion.3
  227.2 0.9 copy.25
  228.1 1.9 fusion.23
  230.0 5.1 collective-permute-start.1
  235.2 3.2 tile.20
  238.3 11.6 %tile.21 = bf16[32,98112]{1,0:T(8,128)(2,1)} reshape(bf16[32,192,511]{2,1,0:T(8,128)(2,1)} %tile.20) | data formatting | bytes 12558336 | tf_op jit(solution)/shard_map/tile | solution.py:19
  249.9 5.8 %slice.122 = bf16[32,97920]{1,0:T(8,128)(2,1)} slice(bf16[32,98112]{1,0:T(8,128)(2,1)} %tile.21), slice={[0:32], [0:97920]} | slice | bytes 12533760 | tf_op jit(solution)/shard_map/slice | solution.py:20
  255.8 15.3 %reshape.52 = bf16[32,192,510]{2,1,0:T(8,128)(2,1)} reshape(bf16[32,97920]{1,0:T(8,128)(2,1)} %slice.122) | data formatting | bytes 12533760 | tf_op jit(solution)/shard_map/reshape | solution.py:20
  271.1 0.0 collective-permute-done.1
  271.1 0.9 copy.27
  272.0 4.2 fusion.1
  276.2 0.9 copy.28
  277.2 1.4 slice_multiply_fusion.10
  278.6 0.1 pad_maximum_fusion.1
  278.7 2.0 collective-permute-start.2
  280.7 1.4 collective-permute-done.2
  282.1 0.1 pad_maximum_fusion
  282.2 0.8 fusion.15
  283.0 0.0 copy-start.1
  283.0 0.6 copy-done.6
  283.6 6.6 %multiply_convert_fusion = bf16[3,512,4096]{2,1,0:T(8,128)(2,1)} fusion(bf16[192,3,512]{2,0,1:T(8,128)(2,1)S(1)} %get-tuple-element.29, bf16[192,4096]{1,0:T(8,128)(2,1)S(1)} %copy-done.6), kind=kOutput, calls=%fused_computation | convolution fusion | flops 2428502016 | bytes 14745600 | tf_op jit(solution)/shard_map/sd,sic->dic/dot_general | solution.py:119
  290.2 16.6 %copy.34 = bf16[4096,1536]{1,0:T(8,128)(2,1)} copy(bf16[4096,1536]{0,1:T(8,128)(2,1)} %bitcast.62) | data formatting | bytes 25165824
  306.8 0.0 reduce-scatter.7.cloned.1.call-update
  306.9 0.3 reduce-scatter.5.cloned.1.call-start
  307.1 0.8 copy-done.2
  307.9 10.0 %fusion = bf16[192,4096]{1,0:T(8,128)(2,1)} fusion(bf16[192,3,512]{2,0,1:T(8,128)(2,1)S(1)} %copy-done.2, bf16[4096,3,512]{2,0,1:T(8,128)(2,1)} %all-gather.5.cloned.1.call-done), kind=kOutput, calls=%fused_computation.2 | convolution fusion | flops 2416705536 | bytes 14745600 | tf_op jit(solution)/shard_map/sic,dic->sd/dot_general | solution.py:114
  317.9 0.0 reduce-scatter.5.cloned.1.call-update
  317.9 0.1 copy.30
  318.1 0.5 reverse
  318.6 0.2 slice.183
  318.8 6.9 %fusion.20 = f32[32,192,511]{2,1,0:T(8,128)} fusion(bf16[32,16,192]{2,1,0:T(8,128)(2,1)S(1)} %bitcast.69, bf16[32,16,319]{2,1,0:T(8,128)(2,1)S(1)} %slice.183), kind=kOutput, calls=%fused_computation.33 | convolution fusion | flops 100466688 | bytes 13081600 | tf_op jit(solution)/shard_map/gcs,gcu->gsu/dot_general | solution.py:83
  325.7 13.2 %reshape.55 = f32[32,98112]{1,0:T(8,128)} reshape(f32[32,192,511]{2,1,0:T(8,128)} %fusion.20) | data formatting | bytes 25116672 | tf_op jit(solution)/shard_map/reshape | solution.py:89
  338.8 11.4 %slice.129 = f32[32,97920]{1,0:T(8,128)} slice(f32[32,98112]{1,0:T(8,128)} %reshape.55), slice={[0:32], [0:97920]} | slice | bytes 25067520 | tf_op jit(solution)/shard_map/slice | solution.py:89
  350.3 15.2 %reshape.56 = f32[32,192,510]{2,1,0:T(8,128)} reshape(f32[32,97920]{1,0:T(8,128)} %slice.129) | data formatting | bytes 25067520 | tf_op jit(solution)/shard_map/reshape | solution.py:89
  365.5 4.4 slice_reduce_fusion
  369.9 127.2 %all-reduce.3 = (bf16[32,128]{1,0:T(8,128)(2,1)S(1)}, bf16[3,3,512]{2,1,0:T(4,128)(2,1)S(1)}) all-reduce(bf16[32,128]{1,0:T(8,128)(2,1)S(1)} %slice_reduce_fusion, bf16[3,3,512]{2,1,0:T(4,128)(2,1)S(1)} %pad_maximum_fusion.3), channel_id=1, replica_groups=mesh['dp'=32,'row'=4,'col'=2] {'dp'}, use_global_device_ids=true, to_apply=%region_3.0 | all-reduce | flops 8704 | bytes 34816 | tf_op jit(solution)/shard_map/psum | solution.py:109
  497.1 0.6 convert_multiply_fusion.3
  497.8 0.6 convert_multiply_fusion.2
  498.4 1.2 copy.35
  499.6 1.1 copy.31
  500.7 32.2 %reduce-scatter.5.cloned.1.call-done = bf16[192,512]{1,0:T(8,128)(2,1)} async-done(((bf16[192,4096]{1,0:T(8,128)(2,1)}), bf16[192,512]{1,0:T(8,128)(2,1)}) %reduce-scatter.5.cloned.1.call-update) | async-done | bytes 196624 | tf_op jit(solution)/shard_map/reduce_scatter | solution.py:115
  (16 shorter events, 0.1 us)
Async XLA Ops:
  7.2 50.3 %all-gather.3.cloned.1.call-start = ((), (), s32[]{:S(2)}) async-start(), calls=%async_computation.2 | async-start | bytes 1769472 | tf_op jit(solution)/shard_map/all_gather | solution.py:44
  7.9 166.7 %all-gather.5.cloned.1.call-start = ((), (), s32[]{:S(2)}) async-start(), calls=%async_computation.3 | async-start | bytes 12976128 | tf_op jit(solution)/shard_map/all_gather | solution.py:45
  8.6 175.9 %copy-start.4 = (bf16[32,128]{1,0:T(8,128)(2,1)S(1)}, bf16[32,128]{1,0:T(8,128)(2,1)}, u32[]{:S(2)}) copy-start(bf16[32,128]{1,0:T(8,128)(2,1)} %param.8) | copy-start | bytes 24580
  8.7 489.7 %reduce-scatter.7.cloned.1.call-start = ((), (), s32[]{:S(2)}) async-start(), calls=%async_computation.5 | async-start | bytes 12976128
  182.4 38.2 %collective-permute-start = (bf16[129,3,512]{2,0,1:T(8,128)(2,1)S(1)}, bf16[129,3,512]{2,0,1:T(8,128)(2,1)S(1)}, u32[]{:S(2)}, u32[]{:S(2)}) collective-permute-start(bf16[129,3,512]{2,0,1:T(8,128)(2,1)S(1)} %slice.112), channel_id=1, source_target_pairs={{0,8},{8,16},{16,24},{24,32},{32,40},{40,48},{48,56},{56,64},{64,7... | collective-permute-start | bytes 1188872 | tf_op jit(solution)/shard_map/ppermute | solution.py:10
  205.3 15.3 %copy-start.5 = (f32[3,3,512]{2,1,0:T(4,128)S(1)}, f32[3,3,512]{2,1,0:T(4,128)}, u32[]{:S(2)}) copy-start(f32[3,3,512]{2,1,0:T(4,128)} %param.7) | copy-start | bytes 55300
  221.5 1.3 copy-start
  223.1 5.1 copy-start.3
  230.0 41.0 %collective-permute-start.1 = (bf16[127,512]{1,0:T(8,128)(2,1)S(1)}, bf16[127,512]{1,0:T(8,128)(2,1)S(1)}, u32[]{:S(2)}, u32[]{:S(2)}) collective-permute-start(bf16[127,512]{1,0:T(8,128)(2,1)S(1)} %slice.121), channel_id=1, source_target_pairs={{8,0},{16,8},{24,16},{32,24},{40,32},{48,40},{56,48},{64,56},{72,6... | collective-permute-start | bytes 390152 | tf_op jit(solution)/shard_map/ppermute | solution.py:10
  278.7 3.4 collective-permute-start.2
  282.2 1.4 copy-start.6
  283.0 7.2 %copy-start.1 = (bf16[192,3,512]{2,0,1:T(8,128)(2,1)}, bf16[192,3,512]{2,0,1:T(8,128)(2,1)S(1)}, u32[]{:S(2)}) copy-start(bf16[192,3,512]{2,0,1:T(8,128)(2,1)S(1)} %get-tuple-element.29) | copy-start | bytes 1769476
  306.8 1.1 copy-start.2
  306.9 226.0 %reduce-scatter.5.cloned.1.call-start = ((), (), s32[]{:S(2)}) async-start(), calls=%async_computation.4 | async-start | bytes 1769472 | tf_op jit(solution)/shard_map/reduce_scatter | solution.py:115
Sparse Core Ops, SparseCore 0:
  9.8 47.6 all-gather.2
  60.2 114.3 all-gather.4
  307.0 175.7 reduce-scatter.6
  485.8 47.0 reduce-scatter.4
where the time goes:
time: 540 us; the launch traced here: 539 us
  waiting for transfers between devices  201 us (37%)
  local copies, waits for them, and re-layouts  137 us (25%)
  blocking collectives  127 us (24%)
  matrix products  39.5 us (7%)
  between operations  14 us (3%)
  other arithmetic  10.9 us (2%)
  starting transfers between devices  9.64 us (2%)
    psum x1, blocking collectives, per_device(): lax.psum(filter_part.astype(jnp.bfloat16), 'dp').astype(jnp.float32)  127 us
    all_gather x1, waiting for transfers between devices, per_device(): full_w = lax.all_gather(in_weight, 'dp', axis=0, tiled=True)  117 us
    all_gather x1, waiting for transfers between devices, per_device(): whole = lax.all_gather(tokens, ('row', 'col'), axis=1, tiled=True)  48.7 us
    reduce_scatter x1, waiting for transfers between devices, per_device(): lax.psum_scatter(partial_in.astype(jnp.bfloat16), ('row', 'col'), scatter...  32.2 us
    reshape x2, local copies, waits for them, and re-layouts, toeplitz(): skewed = tiled[:, :rows * (width - 1)].reshape(groups, rows, width - 1)  30.6 us
    another operation x4, local copies, waits for them, and re-layouts, toeplitz(): tiled = jnp.tile(seed_row, (1, rows))  29.5 us
    reshape x2, local copies, waits for them, and re-layouts, per_device(): pairs.reshape(ngroups, rows * width)[:, :rows * (width - 1)]  28.4 us
    unnamed x19, local copies, waits for them, and re-layouts  22.2 us
  transfers between devices with their start and end apart: 7, of which 4 were waited for; matrix products, arithmetic and copies ran while one was open for 25% of the time, Pallas kernels for 0%

commit v1 on v0

--- a/solution.py
+++ b/solution.py
@@ -41,7 +41,10 @@
     margin = ntaps - 1
     span = rows + margin
     scale = float(rows * lax.axis_size("dp")) ** (-0.5)
-    whole = lax.all_gather(tokens, ("row", "col"), axis=1, tiled=True)
+    whole = jnp.concatenate(
+        lax.all_to_all(jnp.stack([tokens] * lax.axis_size(("row", "col"))), ("row", "col"), 0, 0),
+        axis=1,
+    )
     full_w = lax.all_gather(in_weight, "dp", axis=0, tiled=True)
     mixed_in = jnp.einsum("sd,dic->sic", whole, full_w, preferred_element_type=jnp.float32).astype(
         jnp.bfloat16

time: 540 us -> 498 us (0.922)
  waiting for transfers between devices: 201 us -> 124 us
  blocking collectives: 127 us -> 158 us
    all_gather x1 -> x0, waiting for transfers between devices: 48.7 us -> none  [per_device(): whole = lax.all_gather(tokens, ('row', 'col'), axis=1, tiled=True)]
    all_to_all x0 -> x1, blocking collectives: none -> 30.6 us  [per_device(): lax.all_to_all(jnp.stack([tokens] * lax.axis_size(('row', 'col'))), ('row...]
    all_gather x1, waiting for transfers between devices: 117 us -> 89.6 us  [per_device(): full_w = lax.all_gather(in_weight, 'dp', axis=0, tiled=True)]
  transfers between devices with their start and end apart: 7 -> 6, of which waited for: 4 -> 3; matrix products, arithmetic and copies ran while one was open for 25% -> 28% of each run, Pallas kernels for 0% -> 0%
where the time goes in v1:
time: 498 us; the launch traced here: 497 us
  blocking collectives  158 us (32%)
  local copies, waits for them, and re-layouts  141 us (28%)
  waiting for transfers between devices  124 us (25%)
  matrix products  39.2 us (8%)
  between operations  14 us (3%)
  other arithmetic  10.9 us (2%)
  starting transfers between devices  9.61 us (2%)
    psum x1, blocking collectives, per_device(): lax.psum(filter_part.astype(jnp.bfloat16), 'dp').astype(jnp.float32)  127 us
    all_gather x1, waiting for transfers between devices, per_device(): full_w = lax.all_gather(in_weight, 'dp', axis=0, tiled=True)  89.6 us
    reduce_scatter x1, waiting for transfers between devices, per_device(): lax.psum_scatter(partial_in.astype(jnp.bfloat16), ('row', 'col'), scatter...  32.5 us
    all_to_all x1, blocking collectives, per_device(): lax.all_to_all(jnp.stack([tokens] * lax.axis_size(('row', 'col'))), ('row...  30.6 us
    reshape x2, local copies, waits for them, and re-layouts, toeplitz(): skewed = tiled[:, :rows * (width - 1)].reshape(groups, rows, width - 1)  30.6 us
    another operation x4, local copies, waits for them, and re-layouts, toeplitz(): tiled = jnp.tile(seed_row, (1, rows))  29.5 us
    reshape x2, local copies, waits for them, and re-layouts, per_device(): pairs.reshape(ngroups, rows * width)[:, :rows * (width - 1)]  28.3 us
    unnamed x19, local copies, waits for them, and re-layouts  22.3 us
  transfers between devices with their start and end apart: 6, of which 3 were waited for; matrix products, arithmetic and copies ran while one was open for 28% of the time, Pallas kernels for 0%

profile of v1, /device:TPU:4, one launch (start us, length us, event | category | flops | bytes accessed | tf_op | source)
XLA Modules:
  0.0 496.8 jit_solution(17393841461693125012)
XLA Ops:
  7.2 0.0 all-gather.2.cloned.1.call-start
  7.2 0.7 all-gather.2.cloned.1.call-update
  7.9 0.0 reduce-scatter.7.cloned.1.call-start
  7.9 1.1 stack.35
  9.0 30.6 %all_to_all.5 = bf16[8,192,512]{2,1,0:T(8,128)(2,1)S(1)} all-to-all(bf16[8,192,512]{2,1,0:T(8,128)(2,1)S(1)} %stack.35), channel_id=1, replica_groups=mesh['dp'=32,'row'=4,'col'=2] {'row','col'}, dimensions={0} | all-to-all | bytes 3145728 | tf_op jit(solution)/shard_map/all_to_all | solution.py:45
  39.6 0.9 copy.24
  40.5 2.1 reshape.67
  42.6 89.6 %all-gather.2.cloned.1.call-done = bf16[4096,3,512]{2,0,1:T(8,128)(2,1)} async-done(((bf16[128,3,512]{2,0,1:T(8,128)(2,1)}), bf16[4096,3,512]{2,0,1:T(8,128)(2,1)}) %all-gather.2.cloned.1.call-update) | async-done | bytes 12582928 | tf_op jit(solution)/shard_map/all_gather | solution.py:48
  132.2 7.7 %convolution_convert_fusion = bf16[192,3,512]{2,0,1:T(8,128)(2,1)S(1)} fusion(bf16[192,4096,1]{1,0,2:T(8,128)(2,1)} %reshape.67, bf16[4096,3,512]{2,0,1:T(8,128)(2,1)} %all-gather.2.cloned.1.call-done), kind=kOutput, calls=%fused_computation.13 | convolution fusion | flops 2416214016 | bytes 14745600 | tf_op jit(solution)/shard_map/sd,dic->sic/dot_general | solution.py:49
  139.8 0.1 slice.112
  139.9 2.2 collective-permute-start
  142.1 0.1 rev.6
  142.2 3.2 tile.8
  145.4 11.6 %tile.9 = bf16[32,98112]{1,0:T(8,128)(2,1)} reshape(bf16[32,192,511]{2,1,0:T(8,128)(2,1)} %tile.8) | data formatting | bytes 12558336 | tf_op jit(solution)/shard_map/tile | solution.py:19
  157.0 5.8 %slice.119 = bf16[32,97920]{1,0:T(8,128)(2,1)} slice(bf16[32,98112]{1,0:T(8,128)(2,1)} %tile.9), slice={[0:32], [0:97920]} | slice | bytes 12533760 | tf_op jit(solution)/shard_map/slice | solution.py:20
  162.8 15.3 %reshape.59 = bf16[32,192,510]{2,1,0:T(8,128)(2,1)} reshape(bf16[32,97920]{1,0:T(8,128)(2,1)} %slice.119) | data formatting | bytes 12533760 | tf_op jit(solution)/shard_map/reshape | solution.py:20
  178.1 0.0 collective-permute-done
  178.2 0.3 maximum_convert_fusion
  178.4 0.6 fusion.5
  179.0 1.3 copy-done
  180.3 0.1 fusion.13
  180.4 0.2 copy.25
  180.6 0.0 copy-start.4
  180.6 4.1 fusion.3
  184.7 0.9 copy.26
  185.7 1.9 fusion.17
  187.6 5.1 %collective-permute-start.1 = (bf16[127,512]{1,0:T(8,128)(2,1)S(1)}, bf16[127,512]{1,0:T(8,128)(2,1)S(1)}, u32[]{:S(2)}, u32[]{:S(2)}) collective-permute-start(bf16[127,512]{1,0:T(8,128)(2,1)S(1)} %slice.121), channel_id=1, source_target_pairs={{8,0},{16,8},{24,16},{32,24},{40,32},{48,40},{56,48},{64,56},{72,6... | collective-permute-start | bytes 390152 | tf_op jit(solution)/shard_map/ppermute | solution.py:10
  192.7 3.2 tile.20
  195.9 11.6 %tile.21 = bf16[32,98112]{1,0:T(8,128)(2,1)} reshape(bf16[32,192,511]{2,1,0:T(8,128)(2,1)} %tile.20) | data formatting | bytes 12558336 | tf_op jit(solution)/shard_map/tile | solution.py:19
  207.5 5.8 %slice.122 = bf16[32,97920]{1,0:T(8,128)(2,1)} slice(bf16[32,98112]{1,0:T(8,128)(2,1)} %tile.21), slice={[0:32], [0:97920]} | slice | bytes 12533760 | tf_op jit(solution)/shard_map/slice | solution.py:20
  213.3 15.3 %reshape.62 = bf16[32,192,510]{2,1,0:T(8,128)(2,1)} reshape(bf16[32,97920]{1,0:T(8,128)(2,1)} %slice.122) | data formatting | bytes 12533760 | tf_op jit(solution)/shard_map/reshape | solution.py:20
  228.6 0.0 collective-permute-done.1
  228.7 0.9 copy.28
  229.6 4.2 fusion.1
  233.8 0.9 copy.29
  234.7 1.4 slice_multiply_fusion.10
  236.1 0.1 pad_maximum_fusion.1
  236.2 2.0 collective-permute-start.2
  238.2 1.4 collective-permute-done.2
  239.6 0.1 pad_maximum_fusion
  239.7 0.8 fusion.9
  240.6 0.0 copy-start.2
  240.6 0.6 copy-done.1
  241.1 6.4 %multiply_convert_fusion = bf16[3,512,4096]{2,1,0:T(8,128)(2,1)} fusion(bf16[192,3,512]{2,0,1:T(8,128)(2,1)S(1)} %get-tuple-element.29, bf16[192,4096,1]{1,0,2:T(8,128)(2,1)S(1)} %copy-done.1), kind=kOutput, calls=%fused_computation | convolution fusion | flops 2428502016 | bytes 14745600 | tf_op jit(solution)/shard_map/sd,sic->dic/dot_general | solution.py:122
  247.6 16.7 %copy.35 = bf16[4096,1536]{1,0:T(8,128)(2,1)} copy(bf16[4096,1536]{0,1:T(8,128)(2,1)} %bitcast.58) | data formatting | bytes 25165824
  264.3 0.0 reduce-scatter.7.cloned.1.call-update
  264.3 0.3 reduce-scatter.5.cloned.1.call-start
  264.6 0.8 copy-done.3
  265.3 10.0 %fusion = bf16[192,4096]{1,0:T(8,128)(2,1)} fusion(bf16[192,3,512]{2,0,1:T(8,128)(2,1)S(1)} %copy-done.3, bf16[4096,3,512]{2,0,1:T(8,128)(2,1)} %all-gather.2.cloned.1.call-done), kind=kOutput, calls=%fused_computation.2 | convolution fusion | flops 2416705536 | bytes 14745600 | tf_op jit(solution)/shard_map/sic,dic->sd/dot_general | solution.py:117
  275.3 0.0 reduce-scatter.5.cloned.1.call-update
  275.4 0.1 copy.31
  275.5 0.5 reverse
  276.0 0.2 slice.183
  276.2 6.9 %fusion.14 = f32[32,192,511]{2,1,0:T(8,128)} fusion(bf16[32,16,192]{2,1,0:T(8,128)(2,1)S(1)} %bitcast.66, bf16[32,16,319]{2,1,0:T(8,128)(2,1)S(1)} %slice.183), kind=kOutput, calls=%fused_computation.30 | convolution fusion | flops 100466688 | bytes 13081600 | tf_op jit(solution)/shard_map/gcs,gcu->gsu/dot_general | solution.py:86
  283.1 13.2 %reshape.65 = f32[32,98112]{1,0:T(8,128)} reshape(f32[32,192,511]{2,1,0:T(8,128)} %fusion.14) | data formatting | bytes 25116672 | tf_op jit(solution)/shard_map/reshape | solution.py:92
  296.2 11.4 %slice.129 = f32[32,97920]{1,0:T(8,128)} slice(f32[32,98112]{1,0:T(8,128)} %reshape.65), slice={[0:32], [0:97920]} | slice | bytes 25067520 | tf_op jit(solution)/shard_map/slice | solution.py:92
  307.7 15.2 %reshape.66 = f32[32,192,510]{2,1,0:T(8,128)} reshape(f32[32,97920]{1,0:T(8,128)} %slice.129) | data formatting | bytes 25067520 | tf_op jit(solution)/shard_map/reshape | solution.py:92
  322.9 4.4 slice_reduce_fusion
  327.3 127.0 %all-reduce.3 = (bf16[32,128]{1,0:T(8,128)(2,1)S(1)}, bf16[3,3,512]{2,1,0:T(4,128)(2,1)S(1)}) all-reduce(bf16[32,128]{1,0:T(8,128)(2,1)S(1)} %slice_reduce_fusion, bf16[3,3,512]{2,1,0:T(4,128)(2,1)S(1)} %pad_maximum_fusion.3), channel_id=1, replica_groups=mesh['dp'=32,'row'=4,'col'=2] {'dp'}, use_global_device_ids=true, to_apply=%region_3.0 | all-reduce | flops 8704 | bytes 34816 | tf_op jit(solution)/shard_map/psum | solution.py:112
  454.3 0.6 convert_multiply_fusion.3
  454.9 0.6 convert_multiply_fusion.2
  455.5 1.2 copy.36
  456.8 1.1 copy.32
  457.8 32.5 %reduce-scatter.5.cloned.1.call-done = bf16[192,512]{1,0:T(8,128)(2,1)} async-done(((bf16[192,4096]{1,0:T(8,128)(2,1)}), bf16[192,512]{1,0:T(8,128)(2,1)}) %reduce-scatter.5.cloned.1.call-update) | async-done | bytes 196624 | tf_op jit(solution)/shard_map/reduce_scatter | solution.py:118
  (17 shorter events, 0.1 us)
Async XLA Ops:
  7.2 125.0 %all-gather.2.cloned.1.call-start = ((), (), s32[]{:S(2)}) async-start(), calls=%async_computation.3 | async-start | bytes 12976128 | tf_op jit(solution)/shard_map/all_gather | solution.py:48
  7.9 447.6 %reduce-scatter.7.cloned.1.call-start = ((), (), s32[]{:S(2)}) async-start(), calls=%async_computation.5 | async-start | bytes 12976128
  42.6 99.5 %copy-start.5 = (bf16[32,128]{1,0:T(8,128)(2,1)S(1)}, bf16[32,128]{1,0:T(8,128)(2,1)}, u32[]{:S(2)}) copy-start(bf16[32,128]{1,0:T(8,128)(2,1)} %param.8) | copy-start | bytes 24580
  139.9 38.2 %collective-permute-start = (bf16[129,3,512]{2,0,1:T(8,128)(2,1)S(1)}, bf16[129,3,512]{2,0,1:T(8,128)(2,1)S(1)}, u32[]{:S(2)}, u32[]{:S(2)}) collective-permute-start(bf16[129,3,512]{2,0,1:T(8,128)(2,1)S(1)} %slice.112), channel_id=1, source_target_pairs={{0,8},{8,16},{16,24},{24,32},{32,40},{40,48},{48,56},{56,64},{64,7... | collective-permute-start | bytes 1188872 | tf_op jit(solution)/shard_map/ppermute | solution.py:10
  162.8 15.3 %copy-start.6 = (f32[3,3,512]{2,1,0:T(4,128)S(1)}, f32[3,3,512]{2,1,0:T(4,128)}, u32[]{:S(2)}) copy-start(f32[3,3,512]{2,1,0:T(4,128)} %param.7) | copy-start | bytes 55300
  179.0 1.3 copy-start
  180.6 5.1 %copy-start.4 = (bf16[192,512]{1,0:T(8,128)(2,1)S(1)}, bf16[192,512]{1,0:T(8,128)(2,1)}, u32[]{:S(2)}) copy-start(bf16[192,512]{1,0:T(8,128)(2,1)} %param.9) | copy-start | bytes 589828
  187.6 41.0 %collective-permute-start.1 = (bf16[127,512]{1,0:T(8,128)(2,1)S(1)}, bf16[127,512]{1,0:T(8,128)(2,1)S(1)}, u32[]{:S(2)}, u32[]{:S(2)}) collective-permute-start(bf16[127,512]{1,0:T(8,128)(2,1)S(1)} %slice.121), channel_id=1, source_target_pairs={{8,0},{16,8},{24,16},{32,24},{40,32},{48,40},{56,48},{64,56},{72,6... | collective-permute-start | bytes 390152 | tf_op jit(solution)/shard_map/ppermute | solution.py:10
  236.2 3.4 collective-permute-start.2
  239.7 1.4 copy-start.1
  240.6 7.0 %copy-start.2 = (bf16[192,3,512]{2,0,1:T(8,128)(2,1)}, bf16[192,3,512]{2,0,1:T(8,128)(2,1)S(1)}, u32[]{:S(2)}) copy-start(bf16[192,3,512]{2,0,1:T(8,128)(2,1)S(1)} %get-tuple-element.29) | copy-start | bytes 1769476
  264.3 1.1 copy-start.3
  264.3 226.0 %reduce-scatter.5.cloned.1.call-start = ((), (), s32[]{:S(2)}) async-start(), calls=%async_computation.4 | async-start | bytes 1769472 | tf_op jit(solution)/shard_map/reduce_scatter | solution.py:118
Sparse Core Ops, SparseCore 0:
  10.8 121.3 all-gather.1
  264.4 175.4 reduce-scatter.6
  443.0 47.2 reduce-scatter.4
